TPU v7x, 32 devices: a whole 2x2x4 slice. The times are simulated.
32 devices in a mesh: grp: 2 (over x), seq: 16 (over z, y, core).
Axes of the slice: x: 2, y: 2, z: 4, core: 2. Of those that a mesh axis runs over, the one named last changes fastest.
Arguments:
- hidden: bfloat16 [16384, 4096], P(('grp', 'seq')), parts along dimension 0, may hold values from -6 to 6
- token_ids: int32 [32, 512], P(('grp', 'seq')), parts along dimension 0, may hold values from 0 to 128255, as said below
- upstream: bfloat16 [16384, 1024], P(('grp', 'seq')), parts along dimension 0, may hold values from -6 to 6
- w_value: bfloat16 [4096, 1024], P('seq'), may hold values from -0.09375 to 0.09375
- proj_in: bfloat16 [4096, 64], replicated, may hold values from -0.09375 to 0.09375
- proj_out: bfloat16 [8, 128, 64], replicated, may hold values from -0.5 to 0.5
- in_inverse: float32 [8, 64, 64], replicated
- out_inverse: float32 [8, 64, 64], replicated
- datastore: bfloat16 [1024, 32768], P(('grp', 'seq')), parts along dimension 0
Outputs:
- input_grad: bfloat16 [16384, 4096], P(('grp', 'seq')), parts along dimension 0
- scores: float32 [32, 512], P('grp', 'seq'), parts along dimension 0
There are 2 independent parts, one for each index of `grp`. A program takes and returns all parts, laid end to end along the dimension named above; an argument that names none is the same for every part. Nothing has to cross between parts.
Inputs may be any that keep to these rules, and one draw needn't show every extreme that they name: `token_ids`: each sequence holds its live tokens first, then padding ids 0; at least 128 tokens of every sequence are live and some sequence has no padding.
All inputs are finite; a program needn't handle non-finite values.
Results may differ from a plain program's by a relative error of at most 0.0059.
Values may be sent and summed in bfloat16 or wider, within the bound.
A program may use at most 128 MiB of HBM per device.

v0:
```python
import jax
import jax.numpy as jnp
from jax import lax
from jax.sharding import PartitionSpec as P

KVH = 8
HD = 128
RANK = 64


def on_device(
    hidden, token_ids, upstream, w_value, proj_in, proj_out, in_inverse, out_inverse, datastore
):
    local_queries = token_ids.shape[0]
    seq_tokens = token_ids.shape[1]
    live_mask = (token_ids != 0).reshape(-1, 1).astype(jnp.bfloat16)
    masked = upstream * live_mask
    contract_last = (((1,), (1,)), ((), ()))
    full_weight = lax.all_gather(w_value, "seq", axis=0, tiled=True)
    input_grad = lax.dot_general(
        masked, full_weight, contract_last, preferred_element_type=jnp.float32
    ).astype(jnp.bfloat16)
    left_proj = jnp.dot(hidden, proj_in, preferred_element_type=jnp.float32).astype(jnp.bfloat16)
    cot_heads = masked.reshape(-1, KVH, HD)
    right_proj = jnp.einsum(
        "thd,hdr->thr", cot_heads, proj_out, preferred_element_type=jnp.float32
    ).astype(jnp.bfloat16)
    left_seq = left_proj.reshape(local_queries, seq_tokens, RANK)
    right_seq = right_proj.reshape(local_queries, seq_tokens, KVH, RANK)
    raw_grads = jnp.einsum(
        "qti,qthj->qhij", left_seq, right_seq, preferred_element_type=jnp.float32
    )
    half_way = jnp.einsum("hai,qhij->qhaj", in_inverse, raw_grads, precision=lax.Precision.HIGHEST)
    pre_grads = jnp.einsum("qhaj,hjb->qhab", half_way, out_inverse, precision=lax.Precision.HIGHEST)
    query_grads = pre_grads.astype(jnp.bfloat16).reshape(local_queries, -1)
    raw_scores = lax.dot_general(
        lax.all_gather(query_grads, "seq", axis=0, tiled=True),
        datastore,
        contract_last,
        preferred_element_type=jnp.float32,
    )
    power_local = jnp.sum(raw_scores * raw_scores, axis=1)
    power_sum = lax.psum(power_local, "seq")
    row_total = datastore.shape[0] * lax.axis_size("seq")
    spread = jnp.sqrt(power_sum / row_total + 1e-06)
    return (input_grad, raw_scores / spread[:, None])


def solution(mesh):
    placed = (
        P(("grp", "seq"), None),
        P(("grp", "seq"), None),
        P(("grp", "seq"), None),
        P("seq", None),
        P(),
        P(),
        P(),
        P(),
        P(("grp", "seq"), None),
    )
    return jax.shard_map(
        on_device,
        mesh=mesh,
        in_specs=placed,
        out_specs=(P(("grp", "seq"), None), P("grp", "seq")),
        check_vma=False,
    )
```

profile of v0, /device:TPU:0, one launch (start us, length us, event | category | flops | bytes accessed | tf_op | source)
XLA Modules:
  0.0 152.7 jit_solution(1100063933830969309)
XLA Ops:
  7.2 0.0 copy-start
  7.2 0.0 copy-start.3
  7.2 0.0 copy-start.1
  7.2 0.0 copy-start.2
  7.2 0.0 all-gather.6.cloned.1.call-start
  7.3 0.9 fusion.14
  8.1 3.7 %fusion.4 = bf16[512,64,1]{0,1,2:T(8,128)(2,1)S(1)} fusion(bf16[512,4096]{1,0:T(8,128)(2,1)} %param.9, bf16[4096,64]{0,1:T(8,128)(2,1)} %param.13), kind=kOutput, calls=%fused_computation.9 | convolution fusion | flops 268468224 | bytes 4784128 | tf_op jit(solution)/shard_map/dot_general | solution.py:23
  11.8 0.0 copy-done.3
  11.8 2.0 %fusion.2 = f32[8,64,64]{1,2,0:T(8,128)S(1)} fusion(bf16[512,64,1]{0,1,2:T(8,128)(2,1)S(1)} %fusion.4, bf16[8,128,64]{1,2,0:T(8,128)(2,1)S(1)} %copy-done.3, bf16[512,1024]{1,0:T(8,128)(2,1)} %param.11, bf16[512]{0:T(512)(128)(2,1)S(1)} %fusion.14), kind=kOutput, calls=%fused_computation.5 | convolution fusion | flops 101449728 | bytes 1377280 | tf_op jit(solution)/shard_map/qti,qthj->qhij/dot_general | solution.py:30
  13.8 0.0 copy-done.1
  13.8 0.5 convolution_bitcast_fusion
  14.3 0.0 copy-done.2
  14.3 0.6 fusion.3
  15.0 0.8 reshape.42
  15.7 0.0 all-gather.6.cloned.1.call-update
  15.8 0.0 all-gather.4.cloned.1.call-start
  15.8 0.7 all-gather.4.cloned.1.call-update
  16.5 43.6 %all-gather.6.cloned.1.call-done = bf16[16,1,32768]{2,1,0:T(2,128)(2,1)} async-done(((bf16[1,1,32768]{2,1,0:T(2,128)(2,1)}), bf16[16,1,32768]{2,1,0:T(2,128)(2,1)}) %all-gather.6.cloned.1.call-update) | async-done | bytes 1048592 | tf_op jit(solution)/shard_map/all_gather | solution.py:37
  60.1 0.0 copy-done
  60.1 3.2 %multiply_reduce_fusion = (f32[16]{0:T(128)S(1)}, f32[16,32]{1,0:T(8,128)S(1)}) fusion(bf16[32,32768]{1,0:T(8,128)(2,1)S(1)} %copy-done, bf16[16,1,32768]{2,1,0:T(2,128)(2,1)} %all-gather.6.cloned.1.call-done), kind=kOutput, calls=%fused_computation.18 | convolution fusion | flops 33555440 | bytes 3147840 | tf_op jit(solution)/shard_map/dot_general | solution.py:36
  63.3 32.3 %psum.7 = f32[16]{0:T(128)S(1)} all-reduce(f32[16]{0:T(128)S(1)} %get-tuple-element.2), channel_id=1, replica_groups=mesh['grp'=2,'seq'=16] {'seq'}, use_global_device_ids=true, to_apply=%region_1.0 | all-reduce | flops 16 | bytes 128 | tf_op jit(solution)/shard_map/psum | solution.py:43
  95.6 0.7 broadcast_divide_fusion
  96.3 39.3 %all-gather.4.cloned.1.call-done = bf16[4096,1024]{1,0:T(8,128)(2,1)} async-done(((bf16[256,1024]{1,0:T(8,128)(2,1)}), bf16[4096,1024]{1,0:T(8,128)(2,1)}) %all-gather.4.cloned.1.call-update) | async-done | bytes 8388624 | tf_op jit(solution)/shard_map/all_gather | solution.py:19
  135.6 10.3 %convolution_convert_fusion = bf16[512,4096]{1,0:T(8,128)(2,1)} fusion(bf16[4096,1024]{1,0:T(8,128)(2,1)} %all-gather.4.cloned.1.call-done, bf16[512,1024]{1,0:T(8,128)(2,1)} %param.11, bf16[512]{0:T(512)(128)(2,1)S(1)} %fusion.14), kind=kOutput, calls=%fused_computation | convolution fusion | flops 4297588736 | bytes 13632512 | tf_op jit(solution)/shard_map/dot_general | solution.py:20
  (1 shorter events, 0.0 us)
Async XLA Ops:
  7.2 52.9 %copy-start = (bf16[32,32768]{1,0:T(8,128)(2,1)S(1)}, bf16[32,32768]{1,0:T(8,128)(2,1)}, u32[]{:S(2)}) copy-start(bf16[32,32768]{1,0:T(8,128)(2,1)} %param.17) | copy-start | bytes 6291460
  7.2 4.6 %copy-start.3 = (bf16[8,128,64]{1,2,0:T(8,128)(2,1)S(1)}, bf16[8,128,64]{1,2,0:T(8,128)(2,1)}, u32[]{:S(2)}) copy-start(bf16[8,128,64]{1,2,0:T(8,128)(2,1)} %param.14) | copy-start | bytes 393220
  7.2 6.6 %copy-start.1 = (f32[8,64,64]{2,1,0:T(8,128)S(1)}, f32[8,64,64]{2,1,0:T(8,128)}, u32[]{:S(2)}) copy-start(f32[8,64,64]{2,1,0:T(8,128)} %param.15) | copy-start | bytes 393220
  7.2 7.1 %copy-start.2 = (f32[8,64,64]{2,1,0:T(8,128)S(1)}, f32[8,64,64]{2,1,0:T(8,128)}, u32[]{:S(2)}) copy-start(f32[8,64,64]{2,1,0:T(8,128)} %param.16) | copy-start | bytes 393220
  7.2 52.9 %all-gather.6.cloned.1.call-start = ((), (), s32[]{:S(2)}) async-start(), calls=%async_computation.1 | async-start | bytes 2228224 | tf_op jit(solution)/shard_map/all_gather | solution.py:37
  15.8 119.8 %all-gather.4.cloned.1.call-start = ((), (), s32[]{:S(2)}) async-start(), calls=%async_computation | async-start | bytes 8912896 | tf_op jit(solution)/shard_map/all_gather | solution.py:19
Sparse Core Ops, SparseCore 0:
  15.9 44.1 all-gather.5
  62.3 73.2 all-gather.3
where the time goes:
time: 153 us
  waiting for transfers between devices  83.6 us (55%)
  blocking collectives  32.3 us (21%)
  matrix products  20.3 us (13%)
  between operations  14.1 us (9%)
  other arithmetic  1.55 us (1%)
    all_gather x1, waiting for transfers between devices, on_device(): lax.all_gather(query_grads, 'seq', axis=0, tiled=True)  43.6 us
    all_gather x1, waiting for transfers between devices, on_device(): full_weight = lax.all_gather(w_value, 'seq', axis=0, tiled=True)  39.3 us
    psum x1, blocking collectives, on_device(): power_sum = lax.psum(power_local, 'seq')  32.3 us
    dot_general x1, matrix products, on_device(): lax.dot_general(masked, full_weight, contract_last, preferred_element_typ...  10.3 us
    dot_general x1, matrix products, on_device(): jnp.dot(hidden, proj_in, preferred_element_type=jnp.float32)  3.69 us
    dot_general x1, matrix products, on_device(): lax.dot_general(lax.all_gather(query_grads, 'seq', axis=0, tiled=True), d...  3.16 us
  transfers between devices with their start and end apart: 2, of which 2 were waited for; matrix products, arithmetic and copies ran while one was open for 3% of the time, Pallas kernels for 0%

commit v1 on v0

--- a/solution.py
+++ b/solution.py
@@ -16,7 +16,10 @@
     live_mask = (token_ids != 0).reshape(-1, 1).astype(jnp.bfloat16)
     masked = upstream * live_mask
     contract_last = (((1,), (1,)), ((), ()))
-    full_weight = lax.all_gather(w_value, "seq", axis=0, tiled=True)
+    devices = lax.axis_size("seq")
+    blocks = jnp.stack([w_value for _ in range(devices)])
+    blocks = lax.all_to_all(blocks, "seq", split_axis=0, concat_axis=0)
+    full_weight = jnp.concatenate(blocks, axis=0)
     input_grad = lax.dot_general(
         masked, full_weight, contract_last, preferred_element_type=jnp.float32
     ).astype(jnp.bfloat16)

time: 153 us -> 250 us (1.63)
  the two profiles are of different devices: /device:TPU:0 before, /device:TPU:16 now
where the time goes in v1:
time: 250 us
  waiting for transfers between devices  130 us (52%)
  blocking collectives  71.9 us (29%)
  matrix products  20.2 us (8%)
  between operations  14.1 us (6%)
  starting transfers between devices  6.36 us (3%)
  local copies, waits for them, and re-layouts  6.3 us (3%)
    all_gather x1, waiting for transfers between devices, on_device(): lax.all_gather(query_grads, 'seq', axis=0, tiled=True)  130 us
    psum x1, blocking collectives, on_device(): power_sum = lax.psum(power_local, 'seq')  71.9 us
    dot_general x1, matrix products, on_device(): lax.dot_general(masked, full_weight, contract_last, preferred_element_typ...  10.3 us
    all_to_all x1, starting transfers between devices, on_device(): blocks = lax.all_to_all(blocks, 'seq', split_axis=0, concat_axis=0)  6.32 us
    another operation x1, local copies, waits for them, and re-layouts, on_device(): blocks = jnp.stack([w_value for _ in range(devices)])  5.49 us
  transfers between devices with their start and end apart: 2, of which 1 were waited for; matrix products, arithmetic and copies ran while one was open for 5% of the time, Pallas kernels for 0%

profile of v1, /device:TPU:16, one launch (start us, length us, event | category | flops | bytes accessed | tf_op | source)
XLA Modules:
  0.0 250.1 jit_solution(6358649253408310359)
XLA Ops:
  7.2 0.0 copy-start
  7.2 5.5 %stack.2 = bf16[16,256,1024]{2,1,0:T(8,128)(2,1)} broadcast(bf16[256,1024]{1,0:T(8,128)(2,1)} %param.12), dimensions={1,2} | broadcast | bytes 8912896 | tf_op jit(solution)/shard_map/stack | solution.py:20
  12.7 0.0 copy-start.4
  12.7 0.0 copy-start.1
  12.7 6.3 %all-to-all-start = ((bf16[16,256,1024]{2,1,0:T(8,128)(2,1)}), bf16[16,256,1024]{2,1,0:T(8,128)(2,1)}, u32[]{:S(2)}, u32[]{:S(2)}) async-start(bf16[16,256,1024]{2,1,0:T(8,128)(2,1)} %stack.2), calls=%async_computation | async-start | bytes 16777216 | tf_op jit(solution)/shard_map/all_to_all | solution.py:21
  19.0 0.0 copy-start.5
  19.0 0.0 copy-start.2
  19.0 0.0 copy-start.3
  19.0 0.0 all-gather.3.cloned.1.call-start
  19.1 0.0 copy-done.4
  19.1 0.0 copy-done.1
  19.1 3.7 %fusion.4 = bf16[512,64,1]{0,1,2:T(8,128)(2,1)S(1)} fusion(bf16[512,4096]{1,0:T(8,128)(2,1)} %param.9, bf16[4096,64]{0,1:T(8,128)(2,1)S(1)} %copy-done.1), kind=kOutput, calls=%fused_computation.9 | convolution fusion | flops 268468224 | bytes 4784128 | tf_op jit(solution)/shard_map/dot_general | solution.py:26
  22.8 0.0 copy-done.5
  22.8 2.0 fusion.2
  24.8 0.0 copy-done.2
  24.8 0.5 convolution_bitcast_fusion
  25.3 0.0 copy-done.3
  25.3 0.6 fusion.3
  25.9 0.8 reshape.48
  26.7 0.0 all-gather.3.cloned.1.call-update
  26.7 130.4 %all-gather.3.cloned.1.call-done = bf16[16,1,32768]{2,1,0:T(2,128)(2,1)} async-done(((bf16[1,1,32768]{2,1,0:T(2,128)(2,1)}), bf16[16,1,32768]{2,1,0:T(2,128)(2,1)}) %all-gather.3.cloned.1.call-update) | async-done | bytes 1048592 | tf_op jit(solution)/shard_map/all_gather | solution.py:40
  157.2 0.0 copy-done
  157.2 3.2 %multiply_reduce_fusion = (f32[16]{0:T(128)S(1)}, f32[16,32]{1,0:T(8,128)S(1)}) fusion(bf16[32,32768]{1,0:T(8,128)(2,1)S(1)} %copy-done, bf16[16,1,32768]{2,1,0:T(2,128)(2,1)} %all-gather.3.cloned.1.call-done), kind=kOutput, calls=%fused_computation.18 | convolution fusion | flops 33555440 | bytes 3147840 | tf_op jit(solution)/shard_map/dot_general | solution.py:39
  160.3 71.9 %psum.7 = f32[16]{0:T(128)S(1)} all-reduce(f32[16]{0:T(128)S(1)} %get-tuple-element.2), channel_id=1, replica_groups=mesh['grp'=2,'seq'=16] {'seq'}, use_global_device_ids=true, to_apply=%region_1.0 | all-reduce | flops 16 | bytes 128 | tf_op jit(solution)/shard_map/psum | solution.py:46
  232.3 0.7 broadcast_divide_fusion
  233.0 0.0 all-to-all-done
  233.0 10.3 %convolution_convert_fusion = bf16[512,4096]{1,0:T(8,128)(2,1)} fusion(bf16[4096,1024]{1,0:T(8,128)(2,1)} %bitcast, bf16[512,1024]{1,0:T(8,128)(2,1)} %param.11, bf16[512]{0:T(512)(128)(2,1)S(1)} %fusion.14), kind=kOutput, calls=%fused_computation | convolution fusion | flops 4297588736 | bytes 13632512 | tf_op jit(solution)/shard_map/dot_general | solution.py:23
  (2 shorter events, 0.0 us)
Async XLA Ops:
  7.2 150.0 %copy-start = (bf16[32,32768]{1,0:T(8,128)(2,1)S(1)}, bf16[32,32768]{1,0:T(8,128)(2,1)}, u32[]{:S(2)}) copy-start(bf16[32,32768]{1,0:T(8,128)(2,1)} %param.17) | copy-start | bytes 6291460
  12.7 6.4 %copy-start.4 = (s32[1,512]{1,0:T(1,128)S(1)}, s32[1,512]{1,0:T(1,128)}, u32[]{:S(2)}) copy-start(s32[1,512]{1,0:T(1,128)} %param.10) | copy-start | bytes 6148
  12.7 6.4 %copy-start.1 = (bf16[4096,64]{0,1:T(8,128)(2,1)S(1)}, bf16[4096,64]{0,1:T(8,128)(2,1)}, u32[]{:S(2)}) copy-start(bf16[4096,64]{0,1:T(8,128)(2,1)} %param.13) | copy-start | bytes 1572868
  12.7 220.3 %all-to-all-start = ((bf16[16,256,1024]{2,1,0:T(8,128)(2,1)}), bf16[16,256,1024]{2,1,0:T(8,128)(2,1)}, u32[]{:S(2)}, u32[]{:S(2)}) async-start(bf16[16,256,1024]{2,1,0:T(8,128)(2,1)} %stack.2), calls=%async_computation | async-start | bytes 16777216 | tf_op jit(solution)/shard_map/all_to_all | solution.py:21
  19.0 3.8 %copy-start.5 = (bf16[8,128,64]{1,2,0:T(8,128)(2,1)S(1)}, bf16[8,128,64]{1,2,0:T(8,128)(2,1)}, u32[]{:S(2)}) copy-start(bf16[8,128,64]{1,2,0:T(8,128)(2,1)} %param.14) | copy-start | bytes 393220
  19.0 5.8 %copy-start.2 = (f32[8,64,64]{2,1,0:T(8,128)S(1)}, f32[8,64,64]{2,1,0:T(8,128)}, u32[]{:S(2)}) copy-start(f32[8,64,64]{2,1,0:T(8,128)} %param.15) | copy-start | bytes 393220
  19.0 6.3 %copy-start.3 = (f32[8,64,64]{2,1,0:T(8,128)S(1)}, f32[8,64,64]{2,1,0:T(8,128)}, u32[]{:S(2)}) copy-start(f32[8,64,64]{2,1,0:T(8,128)} %param.16) | copy-start | bytes 393220
  19.0 138.2 %all-gather.3.cloned.1.call-start = ((), (), s32[]{:S(2)}) async-start(), calls=%async_computation.1 | async-start | bytes 2228224 | tf_op jit(solution)/shard_map/all_gather | solution.py:40
Sparse Core Ops, SparseCore 0:
  26.9 130.2 all-gather.2
